TPU v7x, 128 devices: a whole 4x4x4 slice. The times are simulated.
128 devices in a mesh: pts: 16 (over z, y), hrs: 8 (over x, core).
Axes of the slice: x: 4, y: 4, z: 4, core: 2. Of those that a mesh axis runs over, the one named last changes fastest.
Arguments:
- fields: float32 [512, 262144], P(('pts', 'hrs')), may hold values from -2000 to 2000, as said below
- probes: float32 [256, 512], replicated, may hold values from -0.25 to 0.25
Outputs:
- basis_rows: float32 [256, 262144], P(None, ('pts', 'hrs'))
- coeffs: float32 [256, 512], replicated
Inputs may be any that keep to these rules, and one draw needn't show every extreme that they name: `fields`: every hour and every grid point carries its own scale, and the values are real-valued and never all zero.
All inputs are finite; a program needn't handle non-finite values.
Results may differ from a plain program's by a relative error of at most 0.00017.
Values sent between devices are 32-bit elements; how exact they have to be, the bound alone decides.
No kernel may reach another device: no remote copies, remote signals or barrier semaphores. Data moves between devices by JAX's collectives and lax.ppermute only.
A program may use at most 64 MiB of HBM per device.

v0:
```python
import jax
import jax.numpy as jnp
from jax import lax
from jax.sharding import PartitionSpec as P

highest = lax.Precision.HIGHEST


def contract_last(left, right):
    return lax.dot_general(
        left, right, (((1,), (1,)), ((), ())), precision=highest, preferred_element_type=jnp.float32
    )


def on_device(fields, probes):
    n_pts = lax.axis_size("pts")
    n_hrs = lax.axis_size("hrs")
    panels = lax.all_to_all(fields, ("pts", "hrs"), split_axis=1, concat_axis=0, tiled=True)
    n_points = panels.shape[1] * n_pts * n_hrs
    sketched = jnp.dot(probes, panels, precision=highest, preferred_element_type=jnp.float32)
    local_gram = contract_last(sketched, sketched) / n_points
    gram_sum = lax.psum(local_gram, ("pts", "hrs"))
    factor = jnp.linalg.cholesky(gram_sum)
    basis_rows = lax.linalg.triangular_solve(factor, sketched, left_side=True, lower=True)
    coeffs = lax.psum(contract_last(basis_rows, panels) / n_points, ("pts", "hrs"))
    return (basis_rows, coeffs)


def solution(mesh):
    return jax.shard_map(
        on_device,
        mesh=mesh,
        in_specs=(P(("pts", "hrs"), None), P()),
        out_specs=(P(None, ("pts", "hrs")), P()),
        check_vma=False,
    )
```

profile of v0, /device:TPU:1, one launch (start us, length us, event | category | flops | bytes accessed | tf_op | source)
XLA Modules:
  0.0 445.6 jit_solution(2200279935162737825)
XLA Ops:
  7.2 0.0 copy-start
  7.2 0.0 all-reduce.4.cloned.1.call-start
  7.2 64.6 %all_to_all.19 = f32[4,128,2048]{2,0,1:T(4,128)} all-to-all(f32[4,128,2048]{2,0,1:T(4,128)} %bitcast.40), channel_id=1, replica_groups=mesh['pts'=16,'hrs'=8] {'pts','hrs'}, dimensions={1} | all-to-all | bytes 8388608 | tf_op jit(solution)/shard_map/all_to_all | solution.py:18
  71.8 5.3 %all_to_all.17 = f32[512,2048]{1,0:T(8,128)} reshape(f32[128,4,2048]{2,1,0:T(4,128)} %bitcast.39) | data formatting | bytes 8388608 | tf_op jit(solution)/shard_map/all_to_all | solution.py:18
  77.1 0.0 copy-done
  77.1 5.4 %fusion.9 = f32[256,2048]{1,0:T(8,128)S(1)} fusion(f32[256,512]{1,0:T(8,128)S(1)} %copy-done, f32[512,2048]{1,0:T(8,128)} %all_to_all.17), kind=kOutput, calls=%fused_computation.31 | convolution fusion | flops 3221225472 | bytes 6815744 | tf_op jit(solution)/shard_map/dot_general | solution.py:20
  82.6 2.6 convolution_multiply_fusion.1
  85.1 0.0 all-reduce.4.cloned.1.call-update
  85.1 0.2 all-reduce.6.cloned.1.call-start
  85.4 137.0 %all-reduce.4.cloned.1.call-done = f32[256,256]{0,1:T(8,128)} async-done(((f32[256,256]{0,1:T(8,128)}), f32[256,256]{0,1:T(8,128)}) %all-reduce.4.cloned.1.call-update) | async-done | bytes 262160 | tf_op jit(solution)/shard_map/psum | solution.py:22
  222.4 1.1 copy.8
  223.5 1.0 fusion.2
  224.5 11.7 %cholesky.50 = f32[128,128]{1,0:T(8,128)S(1)} custom-call(f32[128,128]{1,0:T(8,128)S(1)} %cholesky.118), custom_call_target="Cholesky" | custom-call | tf_op jit(solution)/shard_map/jit(cholesky)/cholesky | solution.py:23
  236.2 9.8 %custom-call.14 = f32[1,128,128]{1,2,0:T(8,128)S(1)} custom-call(f32[1,128,128]{2,1,0:T(8,128)S(1)} %get-tuple-element.23), custom_call_target="InvertDiagBlocksLowerTriangular" | custom-call | tf_op jit(solution)/shard_map/jit(cholesky)/cholesky | solution.py:23
  246.1 0.2 constant_dynamic-update-slice_fusion.1
  246.3 0.3 convolution_subtract_fusion.1
  246.6 11.7 %cholesky.105 = f32[128,128]{1,0:T(8,128)S(1)} custom-call(f32[128,128]{1,0:T(8,128)S(1)} %convolution_subtract_fusion.1), custom_call_target="Cholesky" | custom-call | tf_op jit(solution)/shard_map/jit(cholesky)/cholesky | solution.py:23
  258.3 0.7 compare_reduce_fusion
  260.3 0.1 triangular_solve.57
  260.4 4.1 while.1
  260.5 0.6 fusion.21
  261.1 1.4 bitcast_dynamic-update-slice_fusion.2
  262.5 0.6 fusion.21
  263.1 1.4 bitcast_dynamic-update-slice_fusion.2
  264.5 19.7 %custom-call.15 = f32[2,128,128]{1,2,0:T(8,128)S(1)} custom-call(f32[2,128,128]{2,1,0:T(8,128)S(1)} %get-tuple-element.9), custom_call_target="InvertDiagBlocksLowerTriangular" | custom-call | tf_op jit(solution)/shard_map/triangular_solve | solution.py:24
  284.1 1.1 fusion
  285.2 1.0 convolution_subtract_fusion
  286.2 1.1 fusion.4
  287.3 0.0 copy-start.1
  287.3 0.1 pad_maximum_fusion
  287.4 2.0 copy-done.1
  289.5 0.0 copy-start.2
  289.5 4.5 %convolution_multiply_fusion = f32[256,512]{1,0:T(8,128)} fusion(f32[256,2048]{1,0:T(8,128)S(1)} %pad_maximum_fusion, f32[512,2048]{1,0:T(8,128)S(1)} %copy-done.1), kind=kOutput, calls=%fused_computation.4 | convolution fusion | flops 3221356544 | bytes 6815744 | tf_op jit(solution)/shard_map/dot_general | solution.py:10
  294.0 0.0 copy-done.2
  294.0 0.0 all-reduce.6.cloned.1.call-update
  294.0 142.8 %all-reduce.6.cloned.1.call-done = f32[256,512]{1,0:T(8,128)} async-done(((f32[256,512]{1,0:T(8,128)}), f32[256,512]{1,0:T(8,128)}) %all-reduce.6.cloned.1.call-update) | async-done | bytes 524304 | tf_op jit(solution)/shard_map/psum | solution.py:25
  436.9 1.9 copy.23
  (9 shorter events, 0.1 us)
Async XLA Ops:
  7.2 70.0 %copy-start = (f32[256,512]{1,0:T(8,128)S(1)}, f32[256,512]{1,0:T(8,128)}, u32[]{:S(2)}) copy-start(f32[256,512]{1,0:T(8,128)} %param.3) | copy-start | bytes 1572868
  7.2 215.2 %all-reduce.4.cloned.1.call-start = ((), (), s32[]{:S(2)}) async-start(), calls=%async_computation.1 | async-start | bytes 524288 | tf_op jit(solution)/shard_map/psum | solution.py:22
  85.1 351.7 %all-reduce.6.cloned.1.call-start = ((), (), s32[]{:S(2)}) async-start(), calls=%async_computation.2 | async-start | bytes 1048576 | tf_op jit(solution)/shard_map/psum | solution.py:25
  287.3 2.2 copy-start.1
  289.5 4.5 %copy-start.2 = (f32[256,2048]{1,0:T(8,128)}, f32[256,2048]{1,0:T(8,128)S(1)}, u32[]{:S(2)}) copy-start(f32[256,2048]{1,0:T(8,128)S(1)} %pad_maximum_fusion) | copy-start | bytes 6291460
Sparse Core Ops, SparseCore 0:
  85.3 137.0 all-reduce.3
  294.1 142.6 all-reduce.5
where the time goes:
time: 446 us
  waiting for transfers between devices  280 us (63%)
  blocking collectives  64.6 us (14%)
  other arithmetic  54.8 us (12%)
  matrix products  16.1 us (4%)
  between operations  15.4 us (3%)
  local copies, waits for them, and re-layouts  14.3 us (3%)
    psum x1, waiting for transfers between devices, on_device(): lax.psum(contract_last(basis_rows, panels) / n_points, ('pts', 'hrs'))  143 us
    psum x1, waiting for transfers between devices, on_device(): gram_sum = lax.psum(local_gram, ('pts', 'hrs'))  137 us
    all_to_all x1, blocking collectives, on_device(): lax.all_to_all(fields, ('pts', 'hrs'), split_axis=1, concat_axis=0, tiled...  64.6 us
    another operation x6, other arithmetic, on_device(): factor = jnp.linalg.cholesky(gram_sum)  34 us
    another operation x4, other arithmetic, on_device(): lax.linalg.triangular_solve(factor, sketched, left_side=True, lower=True)  19.9 us
  transfers between devices with their start and end apart: 2, of which 2 were waited for; matrix products, arithmetic and copies ran while one was open for 0% of the time, Pallas kernels for 0%

commit v1 on v0

--- a/solution.py
+++ b/solution.py
@@ -19,7 +19,7 @@
     n_points = panels.shape[1] * n_pts * n_hrs
     sketched = jnp.dot(probes, panels, precision=highest, preferred_element_type=jnp.float32)
     local_gram = contract_last(sketched, sketched) / n_points
-    gram_sum = lax.psum(local_gram, ("pts", "hrs"))
+    gram_sum = jnp.sum(lax.all_gather(local_gram, ("pts", "hrs")), axis=0)
     factor = jnp.linalg.cholesky(gram_sum)
     basis_rows = lax.linalg.triangular_solve(factor, sketched, left_side=True, lower=True)
     coeffs = lax.psum(contract_last(basis_rows, panels) / n_points, ("pts", "hrs"))

time: 446 us -> 424 us (0.951)
  waiting for transfers between devices: 280 us -> 247 us
  other arithmetic: 54.8 us -> 66.1 us
    psum x1 -> x0, waiting for transfers between devices: 137 us -> none  [on_device(): gram_sum = lax.psum(local_gram, ('pts', 'hrs'))]
    all_gather x0 -> x1, waiting for transfers between devices: none -> 103 us  [on_device(): gram_sum = jnp.sum(lax.all_gather(local_gram, ('pts', 'hrs')), axis=0)]
    reduce_sum x0 -> x1, other arithmetic: none -> 12 us  [on_device(): gram_sum = jnp.sum(lax.all_gather(local_gram, ('pts', 'hrs')), axis=0)]
where the time goes in v1:
time: 424 us; the launch traced here: 423 us
  waiting for transfers between devices  247 us (58%)
  other arithmetic  66.1 us (16%)
  blocking collectives  64.6 us (15%)
  matrix products  16.1 us (4%)
  between operations  15.5 us (4%)
  local copies, waits for them, and re-layouts  13.5 us (3%)
    psum x1, waiting for transfers between devices, on_device(): lax.psum(contract_last(basis_rows, panels) / n_points, ('pts', 'hrs'))  144 us
    all_gather x1, waiting for transfers between devices, on_device(): gram_sum = jnp.sum(lax.all_gather(local_gram, ('pts', 'hrs')), axis=0)  103 us
    all_to_all x1, blocking collectives, on_device(): lax.all_to_all(fields, ('pts', 'hrs'), split_axis=1, concat_axis=0, tiled...  64.6 us
    another operation x6, other arithmetic, on_device(): factor = jnp.linalg.cholesky(gram_sum)  34 us
    another operation x4, other arithmetic, on_device(): lax.linalg.triangular_solve(factor, sketched, left_side=True, lower=True)  20.1 us
    reduce_sum x1, other arithmetic, on_device(): gram_sum = jnp.sum(lax.all_gather(local_gram, ('pts', 'hrs')), axis=0)  12 us
  transfers between devices with their start and end apart: 2, of which 2 were waited for; matrix products, arithmetic and copies ran while one was open for 0% of the time, Pallas kernels for 0%

profile of v1, /device:TPU:1, one launch (start us, length us, event | category | flops | bytes accessed | tf_op | source)
XLA Modules:
  0.0 423.2 jit_solution(15242840674371165724)
XLA Ops:
  7.2 0.0 copy-start
  7.2 0.0 all-gather.3.cloned.1.call-start
  7.2 64.6 %all_to_all.19 = f32[4,128,2048]{2,0,1:T(4,128)} all-to-all(f32[4,128,2048]{2,0,1:T(4,128)} %bitcast.42), channel_id=1, replica_groups=mesh['pts'=16,'hrs'=8] {'pts','hrs'}, dimensions={1} | all-to-all | bytes 8388608 | tf_op jit(solution)/shard_map/all_to_all | solution.py:18
  71.8 5.3 %all_to_all.17 = f32[512,2048]{1,0:T(8,128)} reshape(f32[128,4,2048]{2,1,0:T(4,128)} %bitcast.41) | data formatting | bytes 8388608 | tf_op jit(solution)/shard_map/all_to_all | solution.py:18
  77.2 0.0 copy-done
  77.2 5.4 %fusion.9 = f32[256,2048]{1,0:T(8,128)S(1)} fusion(f32[256,512]{1,0:T(8,128)S(1)} %copy-done, f32[512,2048]{1,0:T(8,128)} %all_to_all.17), kind=kOutput, calls=%fused_computation.31 | convolution fusion | flops 3221225472 | bytes 6815744 | tf_op jit(solution)/shard_map/dot_general | solution.py:20
  82.6 2.6 convolution_multiply_fusion.1
  85.2 0.0 all-gather.3.cloned.1.call-update
  85.2 0.2 all-reduce.3.cloned.1.call-start
  85.4 102.6 %all-gather.3.cloned.1.call-done = f32[32768,256]{1,0:T(8,128)} async-done(((f32[256,256]{1,0:T(8,128)}), f32[32768,256]{1,0:T(8,128)}) %all-gather.3.cloned.1.call-update) | async-done | bytes 33554448 | tf_op jit(solution)/shard_map/all_gather | solution.py:22
  188.0 12.0 %reduce_sum.9 = f32[256,256]{1,0:T(8,128)S(1)} reduce(f32[128,256,256]{2,1,0:T(8,128)} %bitcast.40, f32[]{:T(128)} %constant.77.clone.1), dimensions={0}, to_apply=%region_0.0 | reduce | flops 8323072 | bytes 33816580 | tf_op jit(solution)/shard_map/reduce_sum | solution.py:22
  200.0 0.1 copy.8
  200.2 11.7 %cholesky.50 = f32[128,128]{1,0:T(8,128)S(1)} custom-call(f32[128,128]{1,0:T(8,128)S(1)} %cholesky.118), custom_call_target="Cholesky" | custom-call | tf_op jit(solution)/shard_map/jit(cholesky)/cholesky | solution.py:23
  212.0 9.8 %custom-call.14 = f32[1,128,128]{1,2,0:T(8,128)S(1)} custom-call(f32[1,128,128]{2,1,0:T(8,128)S(1)} %get-tuple-element.23), custom_call_target="InvertDiagBlocksLowerTriangular" | custom-call | tf_op jit(solution)/shard_map/jit(cholesky)/cholesky | solution.py:23
  221.8 0.2 constant_dynamic-update-slice_fusion.1
  222.0 0.3 convolution_subtract_fusion.1
  222.3 11.7 %cholesky.105 = f32[128,128]{1,0:T(8,128)S(1)} custom-call(f32[128,128]{1,0:T(8,128)S(1)} %convolution_subtract_fusion.1), custom_call_target="Cholesky" | custom-call | tf_op jit(solution)/shard_map/jit(cholesky)/cholesky | solution.py:23
  234.0 0.7 compare_reduce_fusion
  236.1 0.1 triangular_solve.57
  236.2 4.1 while.1
  236.2 0.6 fusion.21
  236.8 1.4 bitcast_dynamic-update-slice_fusion.2
  238.3 0.6 fusion.21
  238.9 1.4 bitcast_dynamic-update-slice_fusion.2
  240.3 19.9 %custom-call.15 = f32[2,128,128]{1,2,0:T(8,128)S(1)} custom-call(f32[2,128,128]{2,1,0:T(8,128)S(1)} %get-tuple-element.9), custom_call_target="InvertDiagBlocksLowerTriangular" | custom-call | tf_op jit(solution)/shard_map/triangular_solve | solution.py:24
  260.2 1.1 fusion
  261.3 1.0 convolution_subtract_fusion
  262.3 1.1 fusion.4
  263.4 0.0 copy-start.1
  263.4 0.1 pad_maximum_fusion
  263.5 2.0 copy-done.1
  265.5 0.0 copy-start.2
  265.5 4.5 %convolution_multiply_fusion = f32[256,512]{1,0:T(8,128)} fusion(f32[256,2048]{1,0:T(8,128)S(1)} %pad_maximum_fusion, f32[512,2048]{1,0:T(8,128)S(1)} %copy-done.1), kind=kOutput, calls=%fused_computation.4 | convolution fusion | flops 3221356544 | bytes 6815744 | tf_op jit(solution)/shard_map/dot_general | solution.py:10
  270.1 0.0 copy-done.2
  270.1 0.0 all-reduce.3.cloned.1.call-update
  270.1 144.4 %all-reduce.3.cloned.1.call-done = f32[256,512]{1,0:T(8,128)} async-done(((f32[256,512]{1,0:T(8,128)}), f32[256,512]{1,0:T(8,128)}) %all-reduce.3.cloned.1.call-update) | async-done | bytes 524304 | tf_op jit(solution)/shard_map/psum | solution.py:25
  414.5 1.9 copy.21
  (10 shorter events, 0.2 us)
Async XLA Ops:
  7.2 70.0 %copy-start = (f32[256,512]{1,0:T(8,128)S(1)}, f32[256,512]{1,0:T(8,128)}, u32[]{:S(2)}) copy-start(f32[256,512]{1,0:T(8,128)} %param.3) | copy-start | bytes 1572868
  7.2 180.9 %all-gather.3.cloned.1.call-start = ((), (), s32[]{:S(2)}) async-start(), calls=%async_computation.2 | async-start | bytes 33816576 | tf_op jit(solution)/shard_map/all_gather | solution.py:22
  85.2 329.3 %all-reduce.3.cloned.1.call-start = ((), (), s32[]{:S(2)}) async-start(), calls=%async_computation.1 | async-start | bytes 1048576 | tf_op jit(solution)/shard_map/psum | solution.py:25
  263.4 2.2 copy-start.1
  265.5 4.5 %copy-start.2 = (f32[256,2048]{1,0:T(8,128)}, f32[256,2048]{1,0:T(8,128)S(1)}, u32[]{:S(2)}) copy-start(f32[256,2048]{1,0:T(8,128)S(1)} %pad_maximum_fusion) | copy-start | bytes 6291460
Sparse Core Ops, SparseCore 0:
  85.3 102.6 all-gather.2
  270.2 144.2 all-reduce.2
